TPU v7x, 256 devices: a whole 4x4x8 slice. The times are simulated.
256 devices in a mesh: region: 8 (over x, core), sub: 32 (over y, z).
Axes of the slice: x: 4, y: 4, z: 8, core: 2. Of those that a mesh axis runs over, the one named last changes fastest.
Arguments:
- multipliers: float32 [256, 3, 3, 256], P(('region', 'sub')), may hold values from -6 to 6
- direction: float32 [256, 3, 3, 256], P(('region', 'sub')), may hold values from -12 to 12
- residual: float32 [256, 3, 3, 256], P(('region', 'sub')), may hold values from -12 to 12
- reaction: float32 [256, 16, 256], P(('region', 'sub')), may hold values from 0.1 to 2
- viscosity: float32 [256, 16, 256], P(('region', 'sub')), may hold values from 0.5 to 5
- primal_index: int32 [256, 96], P(('region', 'sub')), may hold values from 17 to 2286, as said below
- region_inverse: float32 [8, 3072, 3072], P('region', 'sub'), as said below
- coarse_map: float32 [256, 96, 384], P(('region', 'sub')), may hold values from -0.4375 to 0.4375
- global_inverse: float32 [384, 384], replicated, as said below
Outputs:
- new_multipliers: float32 [256, 3, 3, 256], P(('region', 'sub'))
- new_residual: float32 [256, 3, 3, 256], P(('region', 'sub'))
- velocity: float32 [256, 3, 16, 256], P(('region', 'sub'))
- pressure: float32 [256, 16, 256], P(('region', 'sub'))
Inputs may be any that keep to these rules, and one draw needn't show every extreme that they name: `primal_index`: each row holds 96 different positions, each in the interior of a face (neither face index 0 nor 16 - 1); every row contains the first such position and the last one. `region_inverse`: each region's matrix is symmetric positive definite. `global_inverse`: symmetric positive definite.
All inputs are finite; a program needn't handle non-finite values.
Results may differ from a plain program's by a relative error of at most 0.0001.
Values sent between devices are 32-bit elements; how exact they have to be, the bound alone decides.
A program may use at most 64 MiB of HBM per device.

v0:
```python
import jax
import jax.numpy as jnp
from jax import lax
from jax.sharding import PartitionSpec as P

DOM_Z = 4
LEVELS = 3
SWEEPS = 1
COARSE_SWEEPS = 8
VCYCLES = 2
damping = 0.8


def shifted_2(x, axis, by):
    count = lax.axis_size(axis)
    return lax.ppermute(x, axis, [(i, (i + by) % count) for i in range(count)])


def operate(field, react, weight, cells):
    width = field.shape[-1]
    padded = jnp.pad(field, ((0, 0), (1, 1), (cells, cells)))
    middle = padded[:, 1:-1]
    position = lax.broadcasted_iota(jnp.int32, (1, 1, width), 2) % cells
    above = jnp.where(position < cells - 1, middle[:, :, cells + 1 : cells + 1 + width], 0.0)
    beneath = jnp.where(position > 0, middle[:, :, cells - 1 : cells - 1 + width], 0.0)
    beside = padded[:, 2:, cells : cells + width] + padded[:, :-2, cells : cells + width]
    beside = beside + middle[:, :, 2 * cells :] + middle[:, :, :width]
    beside = beside + above + beneath
    return react * field + weight * (6.0 * field - beside)


def restrict(array, cells):
    lead = array.shape[:-2]
    depth = array.shape[-2]
    half = cells // 2
    blocks = array.reshape(lead + (depth // 2, 2, half, 2, half, 2)).mean(axis=(-5, -3, -1))
    return blocks.reshape(lead + (depth // 2, half * half))


def prolong(array, cells):
    lead = array.shape[:-2]
    depth = array.shape[-2]
    cubic = array.reshape(lead + (depth, cells, cells))
    grown = jnp.repeat(jnp.repeat(jnp.repeat(cubic, 2, axis=-3), 2, axis=-2), 2, axis=-1)
    return grown.reshape(lead + (2 * depth, 4 * cells * cells))


def relax(field, source, react, weight, cells, count):
    diagonal = react + 6.0 * weight
    for _ in range(count):
        field = field + damping * (source - operate(field, react, weight, cells)) / diagonal
    return field


def vcycle(field, source, reacts, cells, level):
    weight = 0.25**level
    if level == LEVELS - 1:
        return relax(field, source, reacts[level], weight, cells, COARSE_SWEEPS)
    field = relax(field, source, reacts[level], weight, cells, SWEEPS)
    remain = restrict(source - operate(field, reacts[level], weight, cells), cells)
    coarse = vcycle(jnp.zeros_like(remain), remain, reacts, cells // 2, level + 1)
    field = field + prolong(coarse, cells // 2)
    return relax(field, source, reacts[level], weight, cells, SWEEPS)


def local_solve(source, react, cells):
    reacts = [react]
    size_now = cells
    for _ in range(LEVELS - 1):
        reacts.append(restrict(reacts[-1], size_now))
        size_now = size_now // 2
    field = jnp.zeros_like(source)
    for _ in range(VCYCLES):
        field = vcycle(field, source, reacts, cells, 0)
    return field


def face_cells(picked, cells):
    face = cells * cells
    block = picked // (3 * face)
    component = picked // face % 3
    spot = picked % face
    first = spot // cells
    second = spot % cells
    upper = cells - 1
    place = jnp.where(
        block == 0,
        upper * face + spot,
        jnp.where(
            block == 1, first * face + upper * cells + second, first * face + second * cells + upper
        ),
    )
    return component * (cells * face) + place


def body(
    multipliers,
    direction,
    residual,
    reaction,
    viscosity,
    primal_index,
    region_inverse,
    coarse_map,
    global_inverse,
):
    highest = lax.Precision.HIGHEST
    react = reaction[0]
    cells = react.shape[0]
    face = react.shape[1]
    upper_end = cells - 1
    active = direction[0]
    below_x = shifted_2(active[0], "region", 1)
    below_y = shifted_2(active[1], "sub", DOM_Z)
    below_z = shifted_2(active[2], "sub", 1)
    source = jnp.zeros((3, cells, face), jnp.float32)
    source = source.at[:, upper_end, :].add(active[0])
    source = source.at[:, :, face - cells :].add(active[1].reshape(3, cells, cells))
    source = source.at[:, :, upper_end::cells].add(active[2].reshape(3, cells, cells))
    source = source.at[:, 0, :].add(-below_x)
    source = source.at[:, :, :cells].add(-below_y.reshape(3, cells, cells))
    source = source.at[:, :, 0::cells].add(-below_z.reshape(3, cells, cells))
    picked = primal_index[0]
    primal = jnp.take(active.reshape(-1), picked)
    rows = region_inverse[0]
    mapping = coarse_map[0]
    share = jnp.dot(primal, mapping, precision=highest)
    total = lax.psum(share, ("region", "sub"))
    region_part = jnp.dot(
        rows, lax.all_gather(primal, "sub", axis=0, tiled=True), precision=highest
    )
    top = jnp.dot(global_inverse, total, precision=highest)
    lifted = region_part + jnp.dot(mapping, top, precision=highest)
    base = local_solve(source, react, cells)
    spots = face_cells(picked, cells)
    velocity = base.reshape(-1).at[spots].add(lifted).reshape(3, cells, face)
    upper_x = velocity[:, upper_end, :]
    upper_y = velocity[:, :, face - cells :].reshape(3, face)
    upper_z = velocity[:, :, upper_end::cells].reshape(3, face)
    lower_x = velocity[:, 0, :]
    lower_y = velocity[:, :, :cells].reshape(3, face)
    lower_z = velocity[:, :, 0::cells].reshape(3, face)
    squares = jnp.sum(residual[0] * residual[0])
    after_x = shifted_2(lower_x, "region", -1)
    after_y = shifted_2(lower_y, "sub", -DOM_Z)
    after_z = shifted_2(lower_z, "sub", -1)
    jump = jnp.stack([upper_x - after_x, upper_y - after_y, upper_z - after_z])
    curvature, squares_all = lax.psum((jnp.sum(active * jump), squares), ("region", "sub"))
    step_x = jnp.concatenate([velocity[0, 1:], after_x[0][None]], axis=0) - velocity[0]
    step_y = (
        jnp.concatenate([velocity[1][:, cells:], after_y[1].reshape(cells, cells)], axis=1)
        - velocity[1]
    )
    position = lax.broadcasted_iota(jnp.int32, (1, face), 1) % cells
    edge_values = jnp.repeat(after_z[2].reshape(cells, cells), cells, axis=1)
    shifted = jnp.pad(velocity[2][:, 1:], ((0, 0), (0, 1)))
    step_z = jnp.where(position == cells - 1, edge_values, shifted) - velocity[2]
    pressure = -viscosity[0] * (step_x + step_y + step_z)
    alpha = squares_all / curvature
    new_multipliers = (multipliers[0] + alpha * active)[None]
    new_residual = (residual[0] - alpha * jump)[None]
    return (new_multipliers, new_residual, velocity[None], pressure[None])


def solution(mesh):
    in_specs = (
        P(("region", "sub"), None, None, None),
        P(("region", "sub"), None, None, None),
        P(("region", "sub"), None, None, None),
        P(("region", "sub"), None, None),
        P(("region", "sub"), None, None),
        P(("region", "sub"), None),
        P("region", "sub", None),
        P(("region", "sub"), None, None),
        P(),
    )
    out_specs = (
        P(("region", "sub"), None, None, None),
        P(("region", "sub"), None, None, None),
        P(("region", "sub"), None, None, None),
        P(("region", "sub"), None, None),
    )
    return jax.shard_map(body, mesh=mesh, in_specs=in_specs, out_specs=out_specs, check_vma=False)
```

profile of v0, /device:TPU:1, one launch (start us, length us, event | category | flops | bytes accessed | tf_op | source)
XLA Modules:
  0.0 369.7 jit_solution(10086883032054162801)
XLA Ops:
  0.6 0.8 fusion.286
  1.5 2.6 collective-permute-start
  4.1 6.9 %collective-permute-start.1 = (f32[3,256]{1,0:T(4,128)S(1)}, f32[3,256]{1,0:T(4,128)S(1)}, u32[]{:S(2)}, u32[]{:S(2)}) collective-permute-start(f32[3,256]{1,0:T(4,128)S(1)} %bitcast.181), channel_id=1, source_target_pairs={{0,4},{1,5},{2,6},{3,7},{4,8},{5,9},{6,10},{7,11},{8,12},{9,13},{1... | collective-permute-start | bytes 9224 | tf_op jit(solution)/shard_map/ppermute | solution.py:16
  11.0 0.7 collective-permute-start.2
  11.8 0.7 add_bitcast_fusion
  12.5 0.7 broadcast_multiply_fusion.6
  13.2 1.7 reshape_squeeze.17
  15.4 0.3 copy.126
  15.7 0.3 scatter-add.34
  16.5 1.1 gather_fusion
  17.7 0.6 dynamic-slice.29
  19.1 114.8 %all-reduce.28 = f32[3072]{0:T(1024)S(1)} all-reduce(f32[3072]{0:T(1024)S(1)} %fusion.269), channel_id=1, replica_groups=mesh['region'=8,'sub'=32] {'sub'}, use_global_device_ids=true, to_apply=%add.28 | all-reduce | flops 3072 | bytes 24576
  133.8 0.2 convolution_reduce_fusion
  134.0 100.0 %psum.22 = f32[384]{0:T(512)S(1)} all-reduce(f32[384]{0:T(512)S(1)} %convolution_reduce_fusion), channel_id=1, replica_groups=mesh['region'=8,'sub'=32] {'region','sub'}, use_global_device_ids=true, to_apply=%region_10.11 | all-reduce | flops 384 | bytes 3072 | tf_op jit(solution)/shard_map/psum | solution.py:128
  234.1 0.6 multiply_reduce_fusion
  234.7 1.0 fusion.2
  235.7 0.6 convolution_bitcast_fusion
  236.3 0.3 fusion.5
  237.5 1.1 scatter_fusion
  238.6 0.3 copy.129
  239.4 4.3 %scatter-add.44 = f32[3,16,256]{1,0,2:T(4,128)S(1)} dynamic-update-slice(f32[3,16,256]{1,0,2:T(4,128)S(1)} %scatter_fusion, f32[3,1,256]{1,0,2:T(4,128)S(1)} %slice_add_fusion, s32[]{:T(128)} %constant.334.clone.1, s32[]{:T(128)} %constant.334.clone.1, s32[]{:T(128)} %constant.334.clone.1) | dynamic-update-slice | bytes 6148 | tf_op jit(solution)/shard_map/scatter-add | solution.py:120
  243.7 1.1 scatter_fusion.1
  244.8 2.0 fusion.17
  246.9 2.0 add_subtract_fusion.1
  249.0 4.8 %reshape.713 = f32[3,8,2,8,2,8,2]{6,5,4,3,2,1,0:T(8,128)} reshape(f32[3,16,256]{2,1,0:T(8,128)S(1)} %copy.135) | data formatting | bytes 98304 | tf_op jit(solution)/shard_map/reshape | solution.py:36
  253.8 2.2 reduce_sum.73
  256.6 0.5 reshape.714
  257.1 0.2 reduce_sum.75
  259.1 2.1 bitcast_add_fusion.1
  261.2 2.1 divide_add_fusion.2
  263.3 2.1 divide_add_fusion.1
  265.3 2.2 add_subtract_fusion
  267.7 4.8 %reshape.721 = f32[3,8,2,8,2,8,2]{6,5,4,3,2,1,0:T(8,128)} reshape(f32[3,16,256]{2,1,0:T(8,128)S(1)} %copy.147) | data formatting | bytes 98304 | tf_op jit(solution)/shard_map/reshape | solution.py:36
  272.5 2.2 reduce_sum.77
  275.2 0.5 reshape.722
  275.7 0.2 reduce_sum.78
  277.9 2.1 divide_add_fusion
  280.2 1.1 scatter_fusion.2
  281.4 1.1 collective-permute-start.3
  282.9 0.6 broadcast_in_dim_reshape.2
  283.6 1.3 collective-permute-start.5
  285.0 2.1 collective-permute-start.4
  287.8 3.6 collective-permute-done.4
  291.4 0.6 fusion.100
  292.1 74.3 %all-reduce.29 = (f32[]{:T(128)}, f32[]{:T(128)}) all-reduce(f32[]{:T(128)} %multiply_reduce_fusion, f32[]{:T(128)} %fusion.100), channel_id=1, replica_groups=mesh['region'=8,'sub'=32] {'region','sub'}, use_global_device_ids=true, to_apply=%region_1.0 | all-reduce | flops 2 | bytes 16 | tf_op jit(solution)/shard_map/psum | solution.py:148
  367.8 0.6 copy.163
  368.4 0.6 copy.162
  369.0 0.7 fusion.99
  (162 shorter events, 8.9 us)
Async XLA Ops:
  0.6 234.1 %copy-start = (f32[1,96,3072]{2,1,0:T(8,128)S(1)}, f32[1,96,3072]{2,1,0:T(8,128)}, u32[]{:S(2)}) copy-start(f32[1,96,3072]{2,1,0:T(8,128)} %param.23) | copy-start | bytes 3538948
  1.5 237.1 %collective-permute-start = (f32[3,256]{1,0:T(4,128)S(1)}, f32[3,256]{1,0:T(4,128)S(1)}, u32[]{:S(2)}, u32[]{:S(2)}) collective-permute-start(f32[3,256]{1,0:T(4,128)S(1)} %bitcast.182), channel_id=1, source_target_pairs={{0,32},{32,64},{64,96},{96,128},{128,160},{160,192},{192,224},{224... | collective-permute-start | bytes 9224 | tf_op jit(solution)/shard_map/ppermute | solution.py:16
  4.1 234.8 %collective-permute-start.1 = (f32[3,256]{1,0:T(4,128)S(1)}, f32[3,256]{1,0:T(4,128)S(1)}, u32[]{:S(2)}, u32[]{:S(2)}) collective-permute-start(f32[3,256]{1,0:T(4,128)S(1)} %bitcast.181), channel_id=1, source_target_pairs={{0,4},{1,5},{2,6},{3,7},{4,8},{5,9},{6,10},{7,11},{8,12},{9,13},{1... | collective-permute-start | bytes 9224 | tf_op jit(solution)/shard_map/ppermute | solution.py:16
  11.0 228.0 %collective-permute-start.2 = (f32[3,256]{1,0:T(4,128)S(1)}, f32[3,256]{1,0:T(4,128)S(1)}, u32[]{:S(2)}, u32[]{:S(2)}) collective-permute-start(f32[3,256]{1,0:T(4,128)S(1)} %bitcast.180), channel_id=1, source_target_pairs={{0,1},{1,2},{2,3},{3,4},{4,5},{5,6},{6,7},{7,8},{8,9},{9,10},{10,1... | collective-permute-start | bytes 9224 | tf_op jit(solution)/shard_map/ppermute | solution.py:16
  15.1 1.3 copy-start.8
  15.1 1.3 copy-start.4
  15.4 2.3 copy-start.9
  15.4 118.4 %copy-start.2 = (f32[1,96,384]{2,1,0:T(8,128)S(1)}, f32[1,96,384]{2,1,0:T(8,128)}, u32[]{:S(2)}) copy-start(f32[1,96,384]{2,1,0:T(8,128)} %param.24) | copy-start | bytes 442372
  15.6 218.4 %copy-start.5 = (f32[1,3,3,256]{3,0,2,1:T(1,128)S(1)}, f32[1,3,3,256]{3,0,2,1:T(1,128)}, u32[]{:S(2)}) copy-start(f32[1,3,3,256]{3,0,2,1:T(1,128)} %param.19) | copy-start | bytes 27652
  16.0 219.7 %copy-start.1 = (f32[384,384]{1,0:T(8,128)S(1)}, f32[384,384]{1,0:T(8,128)}, u32[]{:S(2)}) copy-start(f32[384,384]{1,0:T(8,128)} %param.25) | copy-start | bytes 1769476
  234.7 2.4 copy-start.3
  280.2 88.2 %copy-start.7 = (f32[1,3,3,256]{3,0,2,1:T(1,128)S(1)}, f32[1,3,3,256]{3,0,2,1:T(1,128)}, u32[]{:S(2)}) copy-start(f32[1,3,3,256]{3,0,2,1:T(1,128)} %param.17) | copy-start | bytes 27652
  280.2 88.8 %copy-start.6 = (f32[1,16,256]{2,1,0:T(8,128)S(1)}, f32[1,16,256]{2,1,0:T(8,128)}, u32[]{:S(2)}) copy-start(f32[1,16,256]{2,1,0:T(8,128)} %param.21) | copy-start | bytes 49156
  281.4 6.0 %collective-permute-start.3 = (f32[3,256]{1,0:T(4,128)S(1)}, f32[3,256]{1,0:T(4,128)S(1)}, u32[]{:S(2)}, u32[]{:S(2)}) collective-permute-start(f32[3,256]{1,0:T(4,128)S(1)} %bitcast.183), channel_id=1, source_target_pairs={{0,224},{32,0},{64,32},{96,64},{128,96},{160,128},{192,160},{224,1... | collective-permute-start | bytes 9224 | tf_op jit(solution)/shard_map/ppermute | solution.py:16
  283.6 3.8 %collective-permute-start.5 = (f32[3,256]{1,0:T(4,128)S(1)}, f32[3,256]{1,0:T(4,128)S(1)}, u32[]{:S(2)}, u32[]{:S(2)}) collective-permute-start(f32[3,256]{1,0:T(4,128)S(1)} %reshape.734), channel_id=1, source_target_pairs={{0,31},{1,0},{2,1},{3,2},{4,3},{5,4},{6,5},{7,6},{8,7},{9,8},{10,9... | collective-permute-start | bytes 9224 | tf_op jit(solution)/shard_map/ppermute | solution.py:16
  285.0 6.4 %collective-permute-start.4 = (f32[3,256]{1,0:T(4,128)S(1)}, f32[3,256]{1,0:T(4,128)S(1)}, u32[]{:S(2)}, u32[]{:S(2)}) collective-permute-start(f32[3,256]{1,0:T(4,128)S(1)} %reshape.732), channel_id=1, source_target_pairs={{0,28},{1,29},{2,30},{3,31},{4,0},{5,1},{6,2},{7,3},{8,4},{9,5},{1... | collective-permute-start | bytes 9224 | tf_op jit(solution)/shard_map/ppermute | solution.py:16
where the time goes:
time: 371 us; the launch traced here: 370 us
  blocking collectives  289 us (78%)
  other arithmetic  29.4 us (8%)
  local copies, waits for them, and re-layouts  27.2 us (7%)
  starting transfers between devices  14.8 us (4%)
    unnamed x1, blocking collectives  115 us
    psum x1, blocking collectives, body(): total = lax.psum(share, ('region', 'sub'))  100 us
    psum x1, blocking collectives, body(): lax.psum((jnp.sum(active * jump), squares), ('region', 'sub'))  74.3 us
    ppermute x6, starting transfers between devices, shifted_2(): return lax.ppermute(x, axis, [(i, (i + by) % count) for i in range(count)])  14.8 us
    reshape x4, local copies, waits for them, and re-layouts, restrict(): array.reshape(lead + (depth // 2, 2, half, 2, half, 2))  10.7 us
    add x17, other arithmetic, relax(): field + damping * (source - operate(field, react, weight, cells)) / diagonal  7.44 us
  transfers between devices with their start and end apart: 6, of which 1 were waited for; matrix products, arithmetic and copies ran while one was open for 4% of the time, Pallas kernels for 0%

commit v1 on v0

--- a/solution.py
+++ b/solution.py
@@ -125,7 +125,9 @@
     rows = region_inverse[0]
     mapping = coarse_map[0]
     share = jnp.dot(primal, mapping, precision=highest)
-    total = lax.psum(share, ("region", "sub"))
+    total = share
+    for mesh_axis in ("region", "sub"):
+        total = lax.psum(total, mesh_axis)
     region_part = jnp.dot(
         rows, lax.all_gather(primal, "sub", axis=0, tiled=True), precision=highest
     )

time: 371 us -> 308 us (0.83)
  blocking collectives: 289 us -> 198 us
  starting transfers between devices: 14.8 us -> 41.3 us
    psum x1, blocking collectives: 100 us -> 11.3 us  [body(): total = lax.psum(total, mesh_axis)]
    ppermute x6, starting transfers between devices: 14.8 us -> 41.3 us  [shifted_2(): return lax.ppermute(x, axis, [(i, (i + by) % count) for i in range(count)])]
  transfers between devices with their start and end apart: 6 -> 6, of which waited for: 1 -> 2; matrix products, arithmetic and copies ran while one was open for 4% -> 4% of each run, Pallas kernels for 0% -> 0%
where the time goes in v1:
time: 308 us; the launch traced here: 307 us
  blocking collectives  198 us (64%)
  starting transfers between devices  41.3 us (13%)
  other arithmetic  29.4 us (10%)
  local copies, waits for them, and re-layouts  27.2 us (9%)
  waiting for transfers between devices  5.68 us (2%)
  between operations  3.48 us (1%)
    unnamed x1, blocking collectives  114 us
    psum x1, blocking collectives, body(): lax.psum((jnp.sum(active * jump), squares), ('region', 'sub'))  72.8 us
    ppermute x6, starting transfers between devices, shifted_2(): return lax.ppermute(x, axis, [(i, (i + by) % count) for i in range(count)])  41.3 us
    psum x1, blocking collectives, body(): total = lax.psum(total, mesh_axis)  11.3 us
    reshape x4, local copies, waits for them, and re-layouts, restrict(): array.reshape(lead + (depth // 2, 2, half, 2, half, 2))  10.7 us
    add x17, other arithmetic, relax(): field + damping * (source - operate(field, react, weight, cells)) / diagonal  7.44 us
  transfers between devices with their start and end apart: 6, of which 2 were waited for; matrix products, arithmetic and copies ran while one was open for 4% of the time, Pallas kernels for 0%

profile of v1, /device:TPU:1, one launch (start us, length us, event | category | flops | bytes accessed | tf_op | source)
XLA Modules:
  0.0 307.4 jit_solution(1538200924350504840)
XLA Ops:
  0.6 0.8 fusion.286
  1.5 2.6 collective-permute-start
  4.1 6.9 %collective-permute-start.1 = (f32[3,256]{1,0:T(4,128)S(1)}, f32[3,256]{1,0:T(4,128)S(1)}, u32[]{:S(2)}, u32[]{:S(2)}) collective-permute-start(f32[3,256]{1,0:T(4,128)S(1)} %bitcast.181), channel_id=1, source_target_pairs={{0,4},{1,5},{2,6},{3,7},{4,8},{5,9},{6,10},{7,11},{8,12},{9,13},{1... | collective-permute-start | bytes 9224 | tf_op jit(solution)/shard_map/ppermute | solution.py:16
  11.0 0.7 collective-permute-start.2
  11.8 0.7 add_bitcast_fusion
  12.5 0.7 broadcast_multiply_fusion.6
  13.2 1.7 reshape_squeeze.17
  15.4 0.3 copy.126
  15.7 0.3 scatter-add.34
  16.5 1.1 gather_fusion
  17.7 0.2 convolution_reduce_fusion
  17.9 11.3 %psum.29 = f32[384]{0:T(512)S(1)} all-reduce(f32[384]{0:T(512)S(1)} %convolution_reduce_fusion), channel_id=1, replica_groups=mesh['region'=8,'sub'=32] {'region'}, use_global_device_ids=true, to_apply=%region_10.11 | all-reduce | flops 384 | bytes 3072 | tf_op jit(solution)/shard_map/psum | solution.py:130
  29.2 0.6 dynamic-slice.29
  30.6 114.1 %all-reduce.30 = (f32[3072]{0:T(1024)S(1)}, f32[384]{0:T(512)S(1)}) all-reduce(f32[3072]{0:T(1024)S(1)} %fusion.269, f32[384]{0:T(512)S(1)} %psum.29), channel_id=1, replica_groups=mesh['region'=8,'sub'=32] {'sub'}, use_global_device_ids=true, to_apply=%add.28 | all-reduce | flops 3456 | bytes 27648
  144.7 0.6 multiply_reduce_fusion
  145.3 0.6 convolution_bitcast_fusion
  145.9 1.1 fusion.2
  147.0 0.2 fusion.5
  148.1 1.1 scatter_fusion
  149.2 0.3 copy.129
  150.0 4.3 %scatter-add.44 = f32[3,16,256]{1,0,2:T(4,128)S(1)} dynamic-update-slice(f32[3,16,256]{1,0,2:T(4,128)S(1)} %scatter_fusion, f32[3,1,256]{1,0,2:T(4,128)S(1)} %slice_add_fusion, s32[]{:T(128)} %constant.334.clone.1, s32[]{:T(128)} %constant.334.clone.1, s32[]{:T(128)} %constant.334.clone.1) | dynamic-update-slice | bytes 6148 | tf_op jit(solution)/shard_map/scatter-add | solution.py:120
  154.3 1.1 scatter_fusion.1
  155.4 2.0 fusion.17
  157.5 2.0 add_subtract_fusion.1
  159.6 4.8 %reshape.713 = f32[3,8,2,8,2,8,2]{6,5,4,3,2,1,0:T(8,128)} reshape(f32[3,16,256]{2,1,0:T(8,128)S(1)} %copy.135) | data formatting | bytes 98304 | tf_op jit(solution)/shard_map/reshape | solution.py:36
  164.5 2.2 reduce_sum.73
  167.2 0.5 reshape.714
  167.7 0.2 reduce_sum.75
  169.7 2.1 bitcast_add_fusion.1
  171.8 2.1 divide_add_fusion.2
  173.9 2.1 divide_add_fusion.1
  175.9 2.2 add_subtract_fusion
  178.3 4.8 %reshape.721 = f32[3,8,2,8,2,8,2]{6,5,4,3,2,1,0:T(8,128)} reshape(f32[3,16,256]{2,1,0:T(8,128)S(1)} %copy.147) | data formatting | bytes 98304 | tf_op jit(solution)/shard_map/reshape | solution.py:36
  183.1 2.2 reduce_sum.77
  185.8 0.5 reshape.722
  186.4 0.2 reduce_sum.78
  188.5 2.1 divide_add_fusion
  190.8 1.1 scatter_fusion.2
  192.0 31.0 %collective-permute-start.3 = (f32[3,256]{1,0:T(4,128)S(1)}, f32[3,256]{1,0:T(4,128)S(1)}, u32[]{:S(2)}, u32[]{:S(2)}) collective-permute-start(f32[3,256]{1,0:T(4,128)S(1)} %bitcast.183), channel_id=1, source_target_pairs={{0,224},{32,0},{64,32},{96,64},{128,96},{160,128},{192,160},{224,1... | collective-permute-start | bytes 9224 | tf_op jit(solution)/shard_map/ppermute | solution.py:16
  223.2 0.2 slice.962
  223.4 0.6 broadcast_in_dim_reshape.2
  224.7 2.0 collective-permute-done.5
  226.9 3.7 %collective-permute-done.4 = f32[3,256]{1,0:T(4,128)S(1)} collective-permute-done((f32[3,256]{1,0:T(4,128)S(1)}, f32[3,256]{1,0:T(4,128)S(1)}, u32[]{:S(2)}, u32[]{:S(2)}) %collective-permute-start.4) | collective-permute-done | bytes 3104 | tf_op jit(solution)/shard_map/ppermute | solution.py:16
  230.7 0.6 fusion.100
  231.4 72.8 %all-reduce.29 = (f32[]{:T(128)}, f32[]{:T(128)}) all-reduce(f32[]{:T(128)} %multiply_reduce_fusion, f32[]{:T(128)} %fusion.100), channel_id=1, replica_groups=mesh['region'=8,'sub'=32] {'region','sub'}, use_global_device_ids=true, to_apply=%region_1.0 | all-reduce | flops 2 | bytes 16 | tf_op jit(solution)/shard_map/psum | solution.py:150
  305.5 0.6 copy.163
  306.1 0.6 copy.162
  306.7 0.7 fusion.99
  (162 shorter events, 8.8 us)
Async XLA Ops:
  0.6 145.3 %copy-start = (f32[1,96,3072]{2,1,0:T(8,128)S(1)}, f32[1,96,3072]{2,1,0:T(8,128)}, u32[]{:S(2)}) copy-start(f32[1,96,3072]{2,1,0:T(8,128)} %param.23) | copy-start | bytes 3538948
  1.5 147.7 %collective-permute-start = (f32[3,256]{1,0:T(4,128)S(1)}, f32[3,256]{1,0:T(4,128)S(1)}, u32[]{:S(2)}, u32[]{:S(2)}) collective-permute-start(f32[3,256]{1,0:T(4,128)S(1)} %bitcast.182), channel_id=1, source_target_pairs={{0,32},{32,64},{64,96},{96,128},{128,160},{160,192},{192,224},{224... | collective-permute-start | bytes 9224 | tf_op jit(solution)/shard_map/ppermute | solution.py:16
  4.1 145.4 %collective-permute-start.1 = (f32[3,256]{1,0:T(4,128)S(1)}, f32[3,256]{1,0:T(4,128)S(1)}, u32[]{:S(2)}, u32[]{:S(2)}) collective-permute-start(f32[3,256]{1,0:T(4,128)S(1)} %bitcast.181), channel_id=1, source_target_pairs={{0,4},{1,5},{2,6},{3,7},{4,8},{5,9},{6,10},{7,11},{8,12},{9,13},{1... | collective-permute-start | bytes 9224 | tf_op jit(solution)/shard_map/ppermute | solution.py:16
  11.0 138.6 %collective-permute-start.2 = (f32[3,256]{1,0:T(4,128)S(1)}, f32[3,256]{1,0:T(4,128)S(1)}, u32[]{:S(2)}, u32[]{:S(2)}) collective-permute-start(f32[3,256]{1,0:T(4,128)S(1)} %bitcast.180), channel_id=1, source_target_pairs={{0,1},{1,2},{2,3},{3,4},{4,5},{5,6},{6,7},{7,8},{8,9},{9,10},{10,1... | collective-permute-start | bytes 9224 | tf_op jit(solution)/shard_map/ppermute | solution.py:16
  15.1 1.3 copy-start.8
  15.1 1.3 copy-start.4
  15.4 2.3 copy-start.2
  15.4 13.9 %copy-start.9 = (u32[256]{0:T(256)S(1)}, u32[256]{0:T(256)}, u32[]{:S(2)}) copy-start(u32[256]{0:T(256)} %constant.426) | copy-start | bytes 3076
  15.6 129.0 %copy-start.5 = (f32[1,3,3,256]{3,0,2,1:T(1,128)S(1)}, f32[1,3,3,256]{3,0,2,1:T(1,128)}, u32[]{:S(2)}) copy-start(f32[1,3,3,256]{3,0,2,1:T(1,128)} %param.19) | copy-start | bytes 27652
  15.7 129.6 %copy-start.1 = (f32[384,384]{1,0:T(8,128)S(1)}, f32[384,384]{1,0:T(8,128)}, u32[]{:S(2)}) copy-start(f32[384,384]{1,0:T(8,128)} %param.25) | copy-start | bytes 1769476
  145.3 2.4 copy-start.3
  190.8 115.3 %copy-start.7 = (f32[1,3,3,256]{3,0,2,1:T(1,128)S(1)}, f32[1,3,3,256]{3,0,2,1:T(1,128)}, u32[]{:S(2)}) copy-start(f32[1,3,3,256]{3,0,2,1:T(1,128)} %param.17) | copy-start | bytes 27652
  190.8 115.9 %copy-start.6 = (f32[1,16,256]{2,1,0:T(8,128)S(1)}, f32[1,16,256]{2,1,0:T(8,128)}, u32[]{:S(2)}) copy-start(f32[1,16,256]{2,1,0:T(8,128)} %param.21) | copy-start | bytes 49156
  192.0 32.6 %collective-permute-start.3 = (f32[3,256]{1,0:T(4,128)S(1)}, f32[3,256]{1,0:T(4,128)S(1)}, u32[]{:S(2)}, u32[]{:S(2)}) collective-permute-start(f32[3,256]{1,0:T(4,128)S(1)} %bitcast.183), channel_id=1, source_target_pairs={{0,224},{32,0},{64,32},{96,64},{128,96},{160,128},{192,160},{224,1... | collective-permute-start | bytes 9224 | tf_op jit(solution)/shard_map/ppermute | solution.py:16
  224.1 2.5 collective-permute-start.5
  224.3 6.4 %collective-permute-start.4 = (f32[3,256]{1,0:T(4,128)S(1)}, f32[3,256]{1,0:T(4,128)S(1)}, u32[]{:S(2)}, u32[]{:S(2)}) collective-permute-start(f32[3,256]{1,0:T(4,128)S(1)} %reshape.732), channel_id=1, source_target_pairs={{0,28},{1,29},{2,30},{3,31},{4,0},{5,1},{6,2},{7,3},{8,4},{9,5},{1... | collective-permute-start | bytes 9224 | tf_op jit(solution)/shard_map/ppermute | solution.py:16
